TPU v7x, 256 devices: a whole 4x4x8 slice. The times are simulated.
256 devices in a mesh: sky: 32 (over z_lo, y, core), edge: 8 (over x, z_hi).
Axes of the slice: x: 4, y: 4, z: 8 (z_hi: 2, z_lo: 4; z = z_hi * 4 + z_lo), core: 2. Of those that a mesh axis runs over, the one named last changes fastest.
Arguments:
- node_feats: bfloat16 [131072, 128], P('sky'), may hold values from -6 to 6
- saved_agg: bfloat16 [131072, 128], P('sky'), may hold values from -9 to 9
- node_cot: bfloat16 [131072, 128], P('sky'), may hold values from -6 to 6
- edge_feats: bfloat16 [2097152, 128], P(('sky', 'edge')), may hold values from -6 to 6
- edge_cot: bfloat16 [2097152, 128], P(('sky', 'edge')), may hold values from -6 to 6
- senders: int32 [2097152], P(('sky', 'edge')), may hold values from 0 to 8191, as said below
- counts: int32 [131072], P('sky'), may hold values from 0 to 16, as said below
- send_lower: int32 [65536], P('sky'), may hold values from 0 to 4095, as said below
- send_upper: int32 [65536], P('sky'), may hold values from 0 to 4095, as said below
- w_recv: bfloat16 [128, 128], replicated, may hold values from -0.3125 to 0.3125
- w_send: bfloat16 [128, 128], replicated, may hold values from -0.3125 to 0.3125
- w_edge: bfloat16 [128, 128], replicated, may hold values from -0.3125 to 0.3125
- w_out: bfloat16 [128, 128], replicated, may hold values from -0.5 to 0.5
- b_edge: float32 [128], replicated, may hold values from -3 to 3
- v_self: bfloat16 [128, 128], replicated, may hold values from -0.375 to 0.375
- v_agg: bfloat16 [128, 128], replicated, may hold values from -0.375 to 0.375
- v_out: bfloat16 [128, 128], replicated, may hold values from -0.5 to 0.5
- b_node: float32 [128], replicated, may hold values from -3 to 3
Outputs:
- node_grad: bfloat16 [131072, 128], P('sky')
- edge_grad: bfloat16 [2097152, 128], P(('sky', 'edge'))
- edge_weight_grads: float32 [4, 128, 128], replicated
- node_weight_grads: float32 [3, 128, 128], replicated
- bias_grads: float32 [2, 128], replicated
Inputs may be any that keep to these rules, and one draw needn't show every extreme that they name: `senders`: A sender below 4096 is a node of the receiver's own tile; from 4096 up it is a halo slot of halo_rows. Dead slots name a sender too. `counts`: counts differ from tile to tile. `send_lower`: each tile's 2048 entries are distinct node rows of that tile. `send_upper`: each tile's 2048 entries are distinct node rows of that tile.
All inputs are finite; a program needn't handle non-finite values.
Results may differ from a plain program's by a relative error of at most 0.012.
Values may be sent and summed in bfloat16 or wider, within the bound.
A program may use at most 128 MiB of HBM per device.

v0:
```python
import jax
import jax.numpy as jnp
from jax import lax
from jax.sharding import PartitionSpec as P

DEGREE = 16


def passed_along(array, axis, by):
    size = lax.axis_size(axis)
    return lax.ppermute(array, axis, [(i, (i + by) % size) for i in range(size)])


def slope(z):
    s = jax.nn.sigmoid(z)
    return s * (1.0 + z * (1.0 - s))


def matmul(a, b):
    return jnp.dot(a, b, preferred_element_type=jnp.float32)


def outer_sum(a, b):
    return jnp.einsum("ef,eg->fg", a, b, preferred_element_type=jnp.float32)


def shards(
    node_feats,
    saved_agg,
    node_cot,
    edge_feats,
    edge_cot,
    senders,
    counts,
    send_lower,
    send_upper,
    w_recv,
    w_send,
    w_edge,
    w_out,
    b_edge,
    v_self,
    v_agg,
    v_out,
    b_node,
):
    nodes = node_feats.shape[0]
    width = node_feats.shape[1]
    halo = send_lower.shape[0]
    groups = lax.axis_size("edge")
    member = lax.axis_index("edge")
    share = nodes // groups
    start = member * share
    upper_rows = jnp.take(node_feats, send_upper, axis=0)
    lower_rows = jnp.take(node_feats, send_lower, axis=0)
    from_lower = passed_along(upper_rows, "sky", 1)
    from_upper = passed_along(lower_rows, "sky", -1)
    all_rows = jnp.concatenate([node_feats, from_lower, from_upper], axis=0)
    own = lax.dynamic_slice_in_dim(node_feats, start, share, 0)
    own_agg = lax.dynamic_slice_in_dim(saved_agg, start, share, 0)
    own_cot = lax.dynamic_slice_in_dim(node_cot, start, share, 0)
    own_counts = lax.dynamic_slice_in_dim(counts, start, share, 0)
    pre_node = matmul(own, v_self) + matmul(own_agg, v_agg) + b_node
    node_act = jax.nn.silu(pre_node).astype(jnp.bfloat16)
    d_pre_node = (matmul(own_cot, v_out.T) * slope(pre_node)).astype(jnp.bfloat16)
    d_agg = matmul(d_pre_node, v_agg.T).astype(jnp.bfloat16)
    d_node = own_cot.astype(jnp.float32) + matmul(d_pre_node, v_self.T)
    sender_rows = jnp.take(all_rows, senders, axis=0)
    pre_edge = (
        jnp.repeat(matmul(own, w_recv), DEGREE, axis=0)
        + matmul(sender_rows, w_send)
        + matmul(edge_feats, w_edge)
        + b_edge
    )
    hidden = jax.nn.silu(pre_edge).astype(jnp.bfloat16)
    live = (
        (jnp.arange(DEGREE, dtype=jnp.int32)[None, :] < own_counts[:, None])
        .astype(jnp.float32)
        .reshape(-1, 1)
    )
    d_msg = (
        (edge_cot.astype(jnp.float32) + jnp.repeat(d_agg.astype(jnp.float32), DEGREE, axis=0))
        * live
    ).astype(jnp.bfloat16)
    d_pre = (matmul(d_msg, w_out.T) * slope(pre_edge)).astype(jnp.bfloat16)
    edge_grad = matmul(d_pre, w_edge.T).astype(jnp.bfloat16)
    to_recv = matmul(d_pre, w_recv.T).reshape(share, DEGREE, width).sum(axis=1)
    to_send = jax.ops.segment_sum(matmul(d_pre, w_send.T), senders, num_segments=nodes + 2 * halo)
    local = to_send[:nodes]
    cot_lower = to_send[nodes : nodes + halo]
    cot_upper = to_send[nodes + halo :]
    back_upper = passed_along(cot_lower.astype(jnp.bfloat16), "sky", -1).astype(cot_lower.dtype)
    back_lower = passed_along(cot_upper.astype(jnp.bfloat16), "sky", 1).astype(cot_upper.dtype)
    local = local.at[send_upper].add(back_upper).at[send_lower].add(back_lower)
    recv_grad = jnp.einsum(
        "nf,nkg->fg", own, d_pre.reshape(share, DEGREE, width), preferred_element_type=jnp.float32
    )
    bias_terms = jnp.stack(
        [
            jnp.sum(d_pre.astype(jnp.float32), axis=0),
            jnp.sum(d_pre_node.astype(jnp.float32), axis=0),
        ]
    )
    terms = jnp.concatenate(
        [
            recv_grad,
            outer_sum(sender_rows, d_pre),
            outer_sum(edge_feats, d_pre),
            outer_sum(hidden, d_msg),
            outer_sum(own, d_pre_node),
            outer_sum(own_agg, d_pre_node),
            outer_sum(node_act, own_cot),
            bias_terms,
        ],
        axis=0,
    )
    used = terms.shape[0]
    chunk = -(-used // (groups * 8)) * 8
    terms = jnp.pad(terms, ((0, chunk * groups - used), (0, 0)))
    terms = lax.psum(terms, "sky")
    mine = lax.dynamic_slice_in_dim(local, start, share, 0) + d_node + to_recv
    local = lax.dynamic_update_slice_in_dim(local, mine, start, 0)
    summed = lax.psum(jnp.concatenate([local, terms], axis=0), "edge")
    node_grad = summed[:nodes].astype(jnp.bfloat16)
    totals = summed[nodes : nodes + used]
    scale = 1.0 / jnp.sqrt(jnp.float32(lax.axis_size("sky") * nodes * DEGREE))
    totals = totals * scale
    blocks = width
    edge_total = totals[: 4 * blocks].reshape(4, blocks, width)
    node_total = totals[4 * blocks : 7 * blocks].reshape(3, blocks, width)
    bias_total = totals[7 * blocks :]
    return (node_grad, edge_grad, edge_total, node_total, bias_total)


def solution(mesh):
    in_specs = (
        P("sky", None),
        P("sky", None),
        P("sky", None),
        P(("sky", "edge"), None),
        P(("sky", "edge"), None),
        P(("sky", "edge")),
        P("sky"),
        P("sky"),
        P("sky"),
        P(),
        P(),
        P(),
        P(),
        P(),
        P(),
        P(),
        P(),
        P(),
    )
    out_specs = (P("sky", None), P(("sky", "edge"), None), P(), P(), P())
    return jax.shard_map(shards, mesh=mesh, in_specs=in_specs, out_specs=out_specs, check_vma=False)
```

profile of v0, /device:TPU:1, one launch (start us, length us, event | category | flops | bytes accessed | tf_op | source)
XLA Modules:
  0.0 690.7 jit_solution(3772573964208403021)
XLA Ops:
  8.8 9.2 %gather_fusion.2 = bf16[2048,128]{1,0:T(8,128)(2,1)} fusion(bf16[4096,128]{1,0:T(8,128)(2,1)} %param.20, s32[2048]{0:T(1024)S(1)} %get-tuple-element.9), kind=kCustom, calls=%fused_computation.1.clone | custom fusion | bytes 1056768 | tf_op jit(solution)/shard_map/jit(_take)/gather | solution.py:55
  17.9 2.2 broadcast_select_fusion.3
  20.1 3.2 collective-permute-start.1
  24.0 8.1 %gather_fusion.1 = bf16[2048,128]{1,0:T(8,128)(2,1)} fusion(bf16[4096,128]{1,0:T(8,128)(2,1)S(1)} %copy-done.1, s32[2048]{0:T(1024)S(1)} %get-tuple-element.11), kind=kCustom, calls=%fused_computation.clone | custom fusion | bytes 1056768 | tf_op jit(solution)/shard_map/jit(_take)/gather | solution.py:54
  32.0 2.2 broadcast_select_fusion.4
  35.5 1.8 convert_reduce_fusion.1
  39.1 1.8 fusion.17
  40.8 1.4 fusion.30
  44.6 1.7 reshape.64
  46.3 3.5 fusion.3
  50.0 1.8 fusion.16
  51.8 2.7 pad_maximum_fusion.1
  54.5 32.8 %gather_fusion = bf16[8192,128]{1,0:T(8,128)(2,1)} fusion(bf16[8192,128]{1,0:T(8,128)(2,1)} %pad_maximum_fusion.1, s32[8192]{0:T(1024)} %fusion.30), kind=kCustom, calls=%fused_computation.2 | custom fusion | bytes 4227072 | tf_op jit(solution)/shard_map/jit(_take)/gather | solution.py:68
  87.5 1.3 copy-done.5
  88.8 2.7 convolution_add_fusion.1
  93.1 2.9 bitcast_reduce_fusion
  96.1 2.6 fusion.14
  99.5 1.9 fusion.6
  101.4 2.7 fusion.44
  104.1 46.5 %scatter_custom_fusion = f32[8192,128]{1,0:T(8,128)} fusion(s32[8192]{0:T(1024)} %param.25, f32[8192,128]{1,0:T(8,128)} %fusion.44, f32[]{:T(128)} %constant.10.clone.1), kind=kCustom, calls=%fused_computation.22 | custom fusion | flops 1048576 | bytes 4194816 | tf_op jit(solution)/shard_map/scatter-add | solution.py:88
  150.5 2.4 convert.9
  154.1 4.8 collective-permute-start.2
  160.2 2.6 concatenate.10
  163.7 3.2 slice.41
  167.7 13.6 %scatter_custom_fusion.1 = f32[4096,128]{1,0:T(8,128)} fusion(f32[4096,128]{1,0:T(8,128)} %slice.41, s32[2048]{0:T(1024)} %get-tuple-element.10, bf16[2048,128]{1,0:T(8,128)(2,1)} %collective-permute-done.2), kind=kCustom, calls=%fused_computation.37 | custom fusion | flops 524288 | bytes 2621440 | tf_op jit(solution)/shard_map/scatter-add | solution.py:94
  181.3 13.6 %scatter_custom_fusion.2 = f32[4096,128]{1,0:T(8,128)} fusion(f32[4096,128]{1,0:T(8,128)} %scatter_custom_fusion.1, s32[2048]{0:T(1024)S(1)} %get-tuple-element.8, bf16[2048,128]{1,0:T(8,128)(2,1)} %collective-permute-done.3), kind=kCustom, calls=%fused_computation.35 | custom fusion | flops 524288 | bytes 2621440 | tf_op jit(solution)/shard_map/scatter-add | solution.py:94
  194.9 1.9 add_dynamic-update-slice_fusion
  196.8 246.4 %all-reduce.4.cloned.1.call-done = f32[960,128]{1,0:T(8,128)} async-done(((f32[960,128]{1,0:T(8,128)}), f32[960,128]{1,0:T(8,128)}) %all-reduce.4.cloned.1.call-update) | async-done | bytes 491536 | tf_op jit(solution)/shard_map/psum | solution.py:120
  443.2 3.4 pad_maximum_fusion
  447.4 3.6 convolution_convert_fusion
  451.0 227.2 %all-reduce.6.cloned.1.call-done = f32[5056,128]{1,0:T(8,128)} async-done(((f32[5056,128]{1,0:T(8,128)}), f32[5056,128]{1,0:T(8,128)}) %all-reduce.6.cloned.1.call-update) | async-done | bytes 2588688 | tf_op jit(solution)/shard_map/psum | solution.py:123
  681.2 2.7 slice.51
  (85 shorter events, 18.3 us)
Async XLA Ops:
  7.2 84.3 %copy-start = (bf16[8192,128]{1,0:T(8,128)(2,1)S(1)}, bf16[8192,128]{1,0:T(8,128)(2,1)}, u32[]{:S(2)}) copy-start(bf16[8192,128]{1,0:T(8,128)(2,1)} %param.23) | copy-start | bytes 6291460
  7.2 436.0 %all-reduce.4.cloned.1.call-start = ((), (), s32[]{:S(2)}) async-start(), calls=%async_computation | async-start | bytes 983040 | tf_op jit(solution)/shard_map/psum | solution.py:120
  8.8 14.5 %copy-start.18 = (s32[2048]{0:T(1024)S(1)}, s32[2048]{0:T(1024)}, u32[]{:S(2)}) copy-start(s32[2048]{0:T(1024)} %param.28) | copy-start | bytes 24580
  8.8 15.2 %copy-start.1 = (bf16[4096,128]{1,0:T(8,128)(2,1)S(1)}, bf16[4096,128]{1,0:T(8,128)(2,1)}, u32[]{:S(2)}) copy-start(bf16[4096,128]{1,0:T(8,128)(2,1)} %param.20) | copy-start | bytes 3145732
  20.1 31.7 %collective-permute-start.1 = (bf16[2048,128]{1,0:T(8,128)(2,1)}, bf16[2048,128]{1,0:T(8,128)(2,1)}, u32[]{:S(2)}, u32[]{:S(2)}) collective-permute-start(bf16[2048,128]{1,0:T(8,128)(2,1)} %broadcast_select_fusion.3), channel_id=1, source_target_pairs={{0,248},{8,0},{16,8},{24,16},{32,24},{40,32},{48,40},{56,48},{64,5... | collective-permute-start | bytes 1572872 | tf_op jit(solution)/shard_map/ppermute | solution.py:11
  23.9 10.3 %copy-start.15 = (bf16[128,128]{1,0:T(8,128)(2,1)S(1)}, bf16[128,128]{1,0:T(8,128)(2,1)}, u32[]{:S(2)}) copy-start(bf16[128,128]{1,0:T(8,128)(2,1)} %param.34) | copy-start | bytes 98308
  23.9 10.4 %copy-start.17 = (bf16[128,128]{1,0:T(8,128)(2,1)S(1)}, bf16[128,128]{1,0:T(8,128)(2,1)}, u32[]{:S(2)}) copy-start(bf16[128,128]{1,0:T(8,128)(2,1)} %param.35) | copy-start | bytes 98308
  24.0 10.4 %copy-start.23 = (f32[128]{0:T(128)S(1)}, f32[128]{0:T(128)}, u32[]{:S(2)}) copy-start(f32[128]{0:T(128)} %param.37) | copy-start | bytes 1540
  32.0 3.5 copy-start.24
  34.2 17.6 %collective-permute-start = (bf16[2048,128]{1,0:T(8,128)(2,1)}, bf16[2048,128]{1,0:T(8,128)(2,1)}, u32[]{:S(2)}, u32[]{:S(2)}) collective-permute-start(bf16[2048,128]{1,0:T(8,128)(2,1)} %broadcast_select_fusion.4), channel_id=1, source_target_pairs={{0,8},{8,16},{16,24},{24,32},{32,40},{40,48},{48,56},{56,64},{64,7... | collective-permute-start | bytes 1572872 | tf_op jit(solution)/shard_map/ppermute | solution.py:11
  35.5 1.8 copy-start.9
  46.3 3.5 copy-start.19
  46.3 3.7 copy-start.10
  87.2 1.6 copy-start.5
  87.2 1.6 copy-start.11
  88.8 2.7 copy-start.12
  88.8 2.7 copy-start.21
  91.5 1.6 copy-start.6
  91.5 1.6 copy-start.25
  96.1 5.3 copy-start.2
  152.9 5.9 copy-start.3
  152.9 7.0 %copy-start.14 = (bf16[512,128]{1,0:T(8,128)(2,1)S(1)}, bf16[512,128]{1,0:T(8,128)(2,1)}, u32[]{:S(2)}) copy-start(bf16[512,128]{1,0:T(8,128)(2,1)} %get-tuple-element.12) | copy-start | bytes 393220
  152.9 7.2 %copy-start.7 = (f32[128,128]{1,0:T(8,128)S(1)}, f32[128,128]{1,0:T(8,128)}, u32[]{:S(2)}) copy-start(f32[128,128]{1,0:T(8,128)} %fusion.22) | copy-start | bytes 196612
  153.0 7.2 %copy-start.8 = (f32[128,128]{1,0:T(8,128)S(1)}, f32[128,128]{1,0:T(8,128)}, u32[]{:S(2)}) copy-start(f32[128,128]{1,0:T(8,128)} %fusion.17) | copy-start | bytes 196612
  153.0 7.2 %copy-start.22 = (f32[128]{0:T(128)S(1)}, f32[128]{0:T(128)}, u32[]{:S(2)}) copy-start(f32[128]{0:T(128)} %get-tuple-element.14) | copy-start | bytes 1540
  154.1 13.6 %collective-permute-start.2 = (bf16[2048,128]{1,0:T(8,128)(2,1)}, bf16[2048,128]{1,0:T(8,128)(2,1)}, u32[]{:S(2)}, u32[]{:S(2)}) collective-permute-start(bf16[2048,128]{1,0:T(8,128)(2,1)} %get-tuple-element.7), channel_id=1, source_target_pairs={{0,248},{8,0},{16,8},{24,16},{32,24},{40,32},{48,40},{56,48},{64,5... | collective-permute-start | bytes 1572872 | tf_op jit(solution)/shard_map/ppermute | solution.py:11
  158.9 22.4 %collective-permute-start.3 = (bf16[2048,128]{1,0:T(8,128)(2,1)}, bf16[2048,128]{1,0:T(8,128)(2,1)}, u32[]{:S(2)}, u32[]{:S(2)}) collective-permute-start(bf16[2048,128]{1,0:T(8,128)(2,1)} %get-tuple-element.6), channel_id=1, source_target_pairs={{0,8},{8,16},{16,24},{24,32},{32,40},{40,48},{48,56},{56,64},{64,7... | collective-permute-start | bytes 1572872 | tf_op jit(solution)/shard_map/ppermute | solution.py:11
  163.7 3.3 copy-start.20
  163.7 514.5 %all-reduce.6.cloned.1.call-start = ((), (), s32[]{:S(2)}) async-start(), calls=%async_computation.1 | async-start | bytes 5177344 | tf_op jit(solution)/shard_map/psum | solution.py:123
  163.7 3.2 copy-start.4
  167.7 27.2 %copy-start.16 = (bf16[128,128]{1,0:T(8,128)(2,1)S(1)}, bf16[128,128]{1,0:T(8,128)(2,1)}, u32[]{:S(2)}) copy-start(bf16[128,128]{1,0:T(8,128)(2,1)} %param.34) | copy-start | bytes 98308
  446.6 0.8 copy-start.13
Sparse Core Ops, SparseCore 0:
  163.8 279.3 all-reduce.3
  446.8 231.3 all-reduce.5
where the time goes:
time: 693 us; the launch traced here: 691 us
  waiting for transfers between devices  474 us (68%)
  other arithmetic  97.3 us (14%)
  local copies, waits for them, and re-layouts  68 us (10%)
  matrix products  29.3 us (4%)
  between operations  14.4 us (2%)
  starting transfers between devices  8.09 us (1%)
    psum x1, waiting for transfers between devices, shards(): terms = lax.psum(terms, 'sky')  246 us
    psum x1, waiting for transfers between devices, shards(): summed = lax.psum(jnp.concatenate([local, terms], axis=0), 'edge')  227 us
    scatter-add x1, other arithmetic, shards(): jax.ops.segment_sum(matmul(d_pre, w_send.T), senders, num_segments=nodes...  46.5 us
    gather x1, local copies, waits for them, and re-layouts, shards(): sender_rows = jnp.take(all_rows, senders, axis=0)  32.8 us
    scatter-add x2, other arithmetic, shards(): local = local.at[send_upper].add(back_upper).at[send_lower].add(back_lower)  27.2 us
    dot_general x12, matrix products, matmul(): return jnp.dot(a, b, preferred_element_type=jnp.float32)  19.3 us
  transfers between devices with their start and end apart: 6, of which 2 were waited for; matrix products, arithmetic and copies ran while one was open for 10% of the time, Pallas kernels for 0%

commit v1 on v0

--- a/solution.py
+++ b/solution.py
@@ -117,7 +117,7 @@
     used = terms.shape[0]
     chunk = -(-used // (groups * 8)) * 8
     terms = jnp.pad(terms, ((0, chunk * groups - used), (0, 0)))
-    terms = lax.psum(terms, "sky")
+    terms = jnp.sum(lax.all_gather(terms, "sky"), axis=0)
     mine = lax.dynamic_slice_in_dim(local, start, share, 0) + d_node + to_recv
     local = lax.dynamic_update_slice_in_dim(local, mine, start, 0)
     summed = lax.psum(jnp.concatenate([local, terms], axis=0), "edge")

time: 693 us -> 470 us (0.68)
  waiting for transfers between devices: 474 us -> 245 us
    psum x1 -> x0, waiting for transfers between devices: 246 us -> none  [shards(): terms = lax.psum(terms, 'sky')]
    ppermute x4, waiting for transfers between devices: 0.01 us -> 12.4 us  [passed_along(): lax.ppermute(array, axis, [(i, (i + by) % size) for i in range(size)])]
  transfers between devices with their start and end apart: 6 -> 6, of which waited for: 2 -> 3; matrix products, arithmetic and copies ran while one was open for 10% -> 25% of each run, Pallas kernels for 0% -> 0%
where the time goes in v1:
time: 470 us; the launch traced here: 468 us
  waiting for transfers between devices  245 us (52%)
  other arithmetic  103 us (22%)
  local copies, waits for them, and re-layouts  66.8 us (14%)
  matrix products  30.2 us (6%)
  between operations  14.3 us (3%)
  starting transfers between devices  8.31 us (2%)
    psum x1, waiting for transfers between devices, shards(): summed = lax.psum(jnp.concatenate([local, terms], axis=0), 'edge')  231 us
    scatter-add x1, other arithmetic, shards(): jax.ops.segment_sum(matmul(d_pre, w_send.T), senders, num_segments=nodes...  46.5 us
    gather x1, local copies, waits for them, and re-layouts, shards(): sender_rows = jnp.take(all_rows, senders, axis=0)  32.5 us
    scatter-add x2, other arithmetic, shards(): local = local.at[send_upper].add(back_upper).at[send_lower].add(back_lower)  26.8 us
    dot_general x12, matrix products, matmul(): return jnp.dot(a, b, preferred_element_type=jnp.float32)  20.2 us
    ppermute x4, waiting for transfers between devices, passed_along(): lax.ppermute(array, axis, [(i, (i + by) % size) for i in range(size)])  12.4 us
    dot_general x6, matrix products, outer_sum(): return jnp.einsum('ef,eg->fg', a, b, preferred_element_type=jnp.float32)  9.72 us
  transfers between devices with their start and end apart: 6, of which 3 were waited for; matrix products, arithmetic and copies ran while one was open for 25% of the time, Pallas kernels for 0%

profile of v1, /device:TPU:1, one launch (start us, length us, event | category | flops | bytes accessed | tf_op | source)
XLA Modules:
  0.0 467.8 jit_solution(6756561519701497759)
XLA Ops:
  8.8 9.2 %gather_fusion.2 = bf16[2048,128]{1,0:T(8,128)(2,1)} fusion(bf16[4096,128]{1,0:T(8,128)(2,1)} %param.20, s32[2048]{0:T(1024)S(1)} %get-tuple-element.9), kind=kCustom, calls=%fused_computation.1.clone | custom fusion | bytes 1056768 | tf_op jit(solution)/shard_map/jit(_take)/gather | solution.py:55
  17.9 2.2 broadcast_select_fusion.3
  20.1 3.2 collective-permute-start.1
  23.9 8.1 %gather_fusion.1 = bf16[2048,128]{1,0:T(8,128)(2,1)} fusion(bf16[4096,128]{1,0:T(8,128)(2,1)S(1)} %copy-done.1, s32[2048]{0:T(1024)S(1)} %get-tuple-element.11), kind=kCustom, calls=%fused_computation.clone | custom fusion | bytes 1056768 | tf_op jit(solution)/shard_map/jit(_take)/gather | solution.py:54
  32.0 2.2 broadcast_select_fusion.4
  35.5 1.8 convert_reduce_fusion.1
  37.2 1.8 fusion.17
  41.5 1.4 fusion.30
  44.5 1.7 reshape.64
  46.2 3.5 fusion.3
  49.9 1.8 fusion.16
  51.7 2.7 pad_maximum_fusion.1
  54.4 32.5 %gather_fusion = bf16[8192,128]{1,0:T(8,128)(2,1)} fusion(bf16[8192,128]{1,0:T(8,128)(2,1)} %pad_maximum_fusion.1, s32[8192]{0:T(1024)} %fusion.30), kind=kCustom, calls=%fused_computation.2 | custom fusion | bytes 4227072 | tf_op jit(solution)/shard_map/jit(_take)/gather | solution.py:68
  88.5 2.7 convolution_add_fusion.1
  92.8 1.9 fusion.6
  94.8 2.3 bitcast_reduce_fusion
  97.1 2.6 fusion.14
  101.9 2.6 concatenate.10
  105.6 4.2 fusion.44
  109.8 46.5 %scatter_custom_fusion = f32[8192,128]{1,0:T(8,128)} fusion(s32[8192]{0:T(1024)} %param.25, f32[8192,128]{1,0:T(8,128)} %fusion.44, f32[]{:T(128)} %constant.10.clone.1), kind=kCustom, calls=%fused_computation.22 | custom fusion | flops 1048576 | bytes 4194816 | tf_op jit(solution)/shard_map/scatter-add | solution.py:88
  156.3 2.6 convert.9
  159.8 4.8 %collective-permute-start.2 = (bf16[2048,128]{1,0:T(8,128)(2,1)S(1)}, bf16[2048,128]{1,0:T(8,128)(2,1)S(1)}, u32[]{:S(2)}, u32[]{:S(2)}) collective-permute-start(bf16[2048,128]{1,0:T(8,128)(2,1)S(1)} %get-tuple-element.7), channel_id=1, source_target_pairs={{0,248},{8,0},{16,8},{24,16},{32,24},{40,32},{48,40},{56,48},{64,5... | collective-permute-start | bytes 1572872 | tf_op jit(solution)/shard_map/ppermute | solution.py:11
  164.6 1.5 slice.41
  167.7 12.4 %collective-permute-done.2 = bf16[2048,128]{1,0:T(8,128)(2,1)S(1)} collective-permute-done((bf16[2048,128]{1,0:T(8,128)(2,1)S(1)}, bf16[2048,128]{1,0:T(8,128)(2,1)S(1)}, u32[]{:S(2)}, u32[]{:S(2)}) %collective-permute-start.2) | collective-permute-done | bytes 524320 | tf_op jit(solution)/shard_map/ppermute | solution.py:11
  180.2 13.4 %scatter_custom_fusion.1 = f32[4096,128]{1,0:T(8,128)} fusion(f32[4096,128]{1,0:T(8,128)} %slice.41, s32[2048]{0:T(1024)} %get-tuple-element.10, bf16[2048,128]{1,0:T(8,128)(2,1)S(1)} %collective-permute-done.2), kind=kCustom, calls=%fused_computation.37 | custom fusion | flops 524288 | bytes 2621440 | tf_op jit(solution)/shard_map/scatter-add | solution.py:94
  193.6 13.3 %scatter_custom_fusion.2 = f32[4096,128]{1,0:T(8,128)} fusion(f32[4096,128]{1,0:T(8,128)} %scatter_custom_fusion.1, s32[2048]{0:T(1024)S(1)} %get-tuple-element.8, bf16[2048,128]{1,0:T(8,128)(2,1)S(1)} %collective-permute-done.3), kind=kCustom, calls=%fused_computation.35 | custom fusion | flops 524288 | bytes 2621440 | tf_op jit(solution)/shard_map/scatter-add | solution.py:94
  207.0 1.9 add_dynamic-update-slice_fusion
  210.1 6.2 %reduce_sum.49 = f32[960,128]{1,0:T(8,128)S(1)} reduce(f32[32,960,128]{2,1,0:T(8,128)} %bitcast.45, f32[]{:T(128)} %constant.10.clone.1), dimensions={0}, to_apply=%region_7.9 | reduce | flops 3809280 | bytes 16220164 | tf_op jit(solution)/shard_map/reduce_sum | solution.py:120
  216.3 3.2 pad_maximum_fusion
  220.3 3.6 convolution_convert_fusion
  223.9 231.3 %all-reduce.3.cloned.1.call-done = f32[5056,128]{1,0:T(8,128)} async-done(((f32[5056,128]{1,0:T(8,128)}), f32[5056,128]{1,0:T(8,128)}) %all-reduce.3.cloned.1.call-update) | async-done | bytes 2588688 | tf_op jit(solution)/shard_map/psum | solution.py:123
  458.3 2.7 slice.51
  (84 shorter events, 21.8 us)
Async XLA Ops:
  7.2 84.0 %copy-start = (bf16[8192,128]{1,0:T(8,128)(2,1)S(1)}, bf16[8192,128]{1,0:T(8,128)(2,1)}, u32[]{:S(2)}) copy-start(bf16[8192,128]{1,0:T(8,128)(2,1)} %param.23) | copy-start | bytes 6291460
  7.2 202.9 %all-gather.3.cloned.1.call-start = ((), (), s32[]{:S(2)}) async-start(), calls=%async_computation.1 | async-start | bytes 16220160 | tf_op jit(solution)/shard_map/all_gather | solution.py:120
  8.8 14.5 %copy-start.17 = (s32[2048]{0:T(1024)S(1)}, s32[2048]{0:T(1024)}, u32[]{:S(2)}) copy-start(s32[2048]{0:T(1024)} %param.28) | copy-start | bytes 24580
  8.8 15.2 %copy-start.1 = (bf16[4096,128]{1,0:T(8,128)(2,1)S(1)}, bf16[4096,128]{1,0:T(8,128)(2,1)}, u32[]{:S(2)}) copy-start(bf16[4096,128]{1,0:T(8,128)(2,1)} %param.20) | copy-start | bytes 3145732
  20.1 31.6 %collective-permute-start.1 = (bf16[2048,128]{1,0:T(8,128)(2,1)}, bf16[2048,128]{1,0:T(8,128)(2,1)}, u32[]{:S(2)}, u32[]{:S(2)}) collective-permute-start(bf16[2048,128]{1,0:T(8,128)(2,1)} %broadcast_select_fusion.3), channel_id=1, source_target_pairs={{0,248},{8,0},{16,8},{24,16},{32,24},{40,32},{48,40},{56,48},{64,5... | collective-permute-start | bytes 1572872 | tf_op jit(solution)/shard_map/ppermute | solution.py:11
  23.9 10.3 %copy-start.14 = (bf16[128,128]{1,0:T(8,128)(2,1)S(1)}, bf16[128,128]{1,0:T(8,128)(2,1)}, u32[]{:S(2)}) copy-start(bf16[128,128]{1,0:T(8,128)(2,1)} %param.34) | copy-start | bytes 98308
  23.9 10.4 %copy-start.16 = (bf16[128,128]{1,0:T(8,128)(2,1)S(1)}, bf16[128,128]{1,0:T(8,128)(2,1)}, u32[]{:S(2)}) copy-start(bf16[128,128]{1,0:T(8,128)(2,1)} %param.35) | copy-start | bytes 98308
  23.9 10.4 %copy-start.22 = (f32[128]{0:T(128)S(1)}, f32[128]{0:T(128)}, u32[]{:S(2)}) copy-start(f32[128]{0:T(128)} %param.37) | copy-start | bytes 1540
  32.0 3.5 copy-start.23
  34.2 17.6 %collective-permute-start = (bf16[2048,128]{1,0:T(8,128)(2,1)}, bf16[2048,128]{1,0:T(8,128)(2,1)}, u32[]{:S(2)}, u32[]{:S(2)}) collective-permute-start(bf16[2048,128]{1,0:T(8,128)(2,1)} %broadcast_select_fusion.4), channel_id=1, source_target_pairs={{0,8},{8,16},{16,24},{24,32},{32,40},{40,48},{48,56},{56,64},{64,7... | collective-permute-start | bytes 1572872 | tf_op jit(solution)/shard_map/ppermute | solution.py:11
  35.5 3.5 copy-start.9
  46.2 3.5 copy-start.18
  46.2 3.7 copy-start.10
  86.9 1.6 copy-start.5
  86.9 1.6 copy-start.11
  88.5 2.7 copy-start.12
  88.5 2.7 copy-start.20
  91.2 1.6 copy-start.6
  92.8 1.9 copy-start.24
  97.1 3.7 copy-start.2
  100.8 1.1 copy-start.7
  100.8 1.1 copy-start.8
  100.8 1.1 copy-start.21
  105.3 350.0 %all-reduce.3.cloned.1.call-start = ((), (), s32[]{:S(2)}) async-start(), calls=%async_computation | async-start | bytes 5177344 | tf_op jit(solution)/shard_map/psum | solution.py:123
  156.3 8.3 %copy-start.4 = (f32[8192,128]{1,0:T(8,128)S(1)}, f32[8192,128]{1,0:T(8,128)}, u32[]{:S(2)}) copy-start(f32[8192,128]{1,0:T(8,128)} %scatter_custom_fusion) | copy-start | bytes 12582916
  159.8 20.4 %collective-permute-start.2 = (bf16[2048,128]{1,0:T(8,128)(2,1)S(1)}, bf16[2048,128]{1,0:T(8,128)(2,1)S(1)}, u32[]{:S(2)}, u32[]{:S(2)}) collective-permute-start(bf16[2048,128]{1,0:T(8,128)(2,1)S(1)} %get-tuple-element.7), channel_id=1, source_target_pairs={{0,248},{8,0},{16,8},{24,16},{32,24},{40,32},{48,40},{56,48},{64,5... | collective-permute-start | bytes 1572872 | tf_op jit(solution)/shard_map/ppermute | solution.py:11
  164.6 2.4 copy-start.3
  164.6 2.4 copy-start.19
  164.6 29.0 %collective-permute-start.3 = (bf16[2048,128]{1,0:T(8,128)(2,1)}, bf16[2048,128]{1,0:T(8,128)(2,1)S(1)}, u32[]{:S(2)}, u32[]{:S(2)}) collective-permute-start(bf16[2048,128]{1,0:T(8,128)(2,1)} %get-tuple-element.6), channel_id=1, source_target_pairs={{0,8},{8,16},{16,24},{24,32},{32,40},{40,48},{48,56},{56,64},{64,7... | collective-permute-start | bytes 1572872 | tf_op jit(solution)/shard_map/ppermute | solution.py:11
  193.6 13.4 %copy-start.15 = (bf16[128,128]{1,0:T(8,128)(2,1)S(1)}, bf16[128,128]{1,0:T(8,128)(2,1)}, u32[]{:S(2)}) copy-start(bf16[128,128]{1,0:T(8,128)(2,1)} %param.34) | copy-start | bytes 98308
  219.5 0.8 copy-start.13
Sparse Core Ops, SparseCore 0:
  105.4 104.6 all-gather.2
  219.7 235.5 all-reduce.2
